TPU v7x, 32 devices: a whole 2x2x4 slice. The times are simulated.
32 devices in a mesh: blk: 8 (over z, y), line: 4 (over x, core).
Axes of the slice: x: 2, y: 2, z: 4, core: 2. Of those that a mesh axis runs over, the one named last changes fastest.
Arguments:
- density: float32 [8, 64, 4096], P('blk', 'line'), may hold values from 0.5 to 1.5
- momentum: float32 [8, 3, 64, 4096], P('blk', None, 'line'), may hold values from -0.5 to 0.5
- energy: float32 [8, 64, 4096], P('blk', 'line'), may hold values from 2 to 4
- adjoint: float32 [8, 5, 64, 4096], P('blk', None, 'line'), may hold values from -6 to 6
- partners: int32 [8, 4], P('blk'), may hold values from 0 to 7
- counts: int32 [8], P('blk'), may hold values from 1 to 4, as said below
- orient: int32 [8, 4], P('blk'), may hold values from 0 to 1
Outputs:
- residual: float32 [8, 5, 64, 4096], P('blk', None, 'line')
- correction: float32 [8], P('blk')
Inputs may be any that keep to these rules, and one draw needn't show every extreme that they name: `partners`: slots at or past counts[b] are padding and are not read. `counts`: some block lists 4 partners.
All inputs are finite; a program needn't handle non-finite values.
Results may differ from a plain program's by a relative error of at most 0.0003.
Values sent between devices are 32-bit elements; how exact they have to be, the bound alone decides.
No kernel may reach another device: no remote copies, remote signals or barrier semaphores. Data moves between devices by JAX's collectives and lax.ppermute only.
A program may use at most 64 MiB of HBM per device.

v0:
```python
import jax
import jax.numpy as jnp
from jax import lax
from jax.sharding import PartitionSpec as P

stencil_one = 0.75
stencil_two = -0.15
stencil_three = 1.0 / 60.0
gamma_less = 0.4
viscosity = 0.5
conduction = 1.5
penalty = 4.0


def difference(fields, direction, start_row, extent):
    length = fields.shape[direction]

    def shifted(offset):
        return lax.slice_in_dim(fields, 3 + offset, length - 3 + offset, axis=direction)

    shape_list = [1] * fields.ndim
    shape_list[direction] = length - 6
    global_row = (start_row + 3 + jnp.arange(length - 6, dtype=jnp.int32)).reshape(shape_list)
    central_one = shifted(1) - shifted(-1)
    central_two = shifted(2) - shifted(-2)
    central_three = shifted(3) - shifted(-3)
    interior = stencil_one * central_one + stencil_two * central_two + stencil_three * central_three
    fourth = 2.0 / 3.0 * central_one - 1.0 / 12.0 * central_two
    second = 0.5 * central_one
    forward = shifted(1) - shifted(0)
    backward = shifted(0) - shifted(-1)
    result = jnp.where((global_row == 2) | (global_row == extent - 3), fourth, interior)
    result = jnp.where((global_row == 1) | (global_row == extent - 2), second, result)
    result = jnp.where(global_row == 0, forward, result)
    result = jnp.where(global_row == extent - 1, backward, result)
    return result


def primitives(fields):
    density_raw = fields[:, 0:1]
    density_safe = jnp.where(density_raw == 0.0, 1.0, density_raw)
    velocity = fields[:, 1:4] / density_safe
    kinetic = 0.5 * jnp.sum(fields[:, 1:4] * velocity, axis=1, keepdims=True)
    pressure = gamma_less * (fields[:, 4:5] - kinetic)
    return (velocity, pressure, density_safe)


def direction_residual(fields, direction, start_row, extent, normal_index):
    velocity, pressure, density_safe = primitives(fields)
    primitive = jnp.concatenate([velocity, pressure / density_safe], axis=1)
    gradient = difference(primitive, direction, start_row, extent)
    length = fields.shape[direction]
    middle = lax.slice_in_dim(fields, 3, length - 3, axis=direction)
    mid_velocity = lax.slice_in_dim(velocity, 3, length - 3, axis=direction)
    mid_pressure = lax.slice_in_dim(pressure, 3, length - 3, axis=direction)
    normal_speed = mid_velocity[:, normal_index : normal_index + 1]
    selector = (jnp.arange(3) == normal_index).astype(fields.dtype).reshape(1, 3, 1, 1)
    convective = jnp.concatenate(
        [
            middle[:, normal_index + 1 : normal_index + 2],
            middle[:, 1:4] * normal_speed + mid_pressure * selector,
            (middle[:, 4:5] + mid_pressure) * normal_speed,
        ],
        axis=1,
    )
    viscous = jnp.concatenate(
        [
            jnp.zeros_like(normal_speed),
            viscosity * gradient[:, 0:3],
            viscosity * conduction * gradient[:, 3:4],
        ],
        axis=1,
    )
    return difference(convective - viscous, direction, start_row + 3, extent)


def per_device(density, momentum, energy, adjoint, partners, counts, orient):
    state = jnp.concatenate([density[:, None], momentum, energy[:, None]], axis=1)
    xrows = state.shape[2]
    yextent = state.shape[3]
    line_count = lax.axis_size("line")
    block_count = lax.axis_size("blk")
    xextent = xrows * line_count
    lines = lax.all_to_all(state, "line", split_axis=3, concat_axis=2, tiled=True)
    padded_lines = jnp.pad(lines, ((0, 0), (0, 0), (6, 6), (0, 0)))
    line_part = direction_residual(padded_lines, 2, -6, xextent, 0)
    xpart = lax.all_to_all(line_part, "line", split_axis=2, concat_axis=3, tiled=True)
    padded_y = jnp.pad(state, ((0, 0), (0, 0), (0, 0), (6, 6)))
    ypart = direction_residual(padded_y, 3, -6, yextent, 1)
    result = xpart + ypart
    bottom_row = state[:, :, :, 0]
    gathered = lax.all_gather(bottom_row, "blk", axis=0, tiled=True)
    slots = jnp.arange(partners.shape[1], dtype=jnp.int32)
    listed = partners[0]
    count_here = counts[0]
    weights = jnp.where(slots < count_here, 1.0 / count_here.astype(jnp.float32), jnp.float32(0.0))
    onehot = (listed[:, None] == jnp.arange(block_count, dtype=jnp.int32)[None, :]).astype(
        jnp.float32
    ) * weights[:, None]
    picked = jnp.einsum("kb,bvx->kvx", onehot, gathered, precision=lax.Precision.HIGHEST)
    signs = (
        jnp.ones((partners.shape[1], 5), jnp.float32)
        .at[:, 2]
        .set(1.0 - 2.0 * orient[0].astype(jnp.float32))
    )
    target = jnp.sum(picked * signs[:, :, None], axis=0)[None]
    result = result.at[:, :, :, yextent - 1].add(penalty * (state[:, :, :, yextent - 1] - target))
    total = lax.psum(jnp.sum(adjoint * result), "line")
    correction = (total / (xextent * yextent)).reshape(1)
    return (result, correction)


def solution(mesh):
    return jax.shard_map(
        per_device,
        mesh=mesh,
        in_specs=(
            P("blk", "line", None),
            P("blk", None, "line", None),
            P("blk", "line", None),
            P("blk", None, "line", None),
            P("blk", None),
            P("blk"),
            P("blk", None),
        ),
        out_specs=(P("blk", None, "line", None), P("blk")),
        check_vma=False,
    )
```

profile of v0, /device:TPU:0, one launch (start us, length us, event | category | flops | bytes accessed | tf_op | source)
XLA Modules:
  0.0 212.0 jit_solution(9206048323847633590)
XLA Ops:
  0.6 1.4 pad_maximum_fusion
  2.0 14.9 %copy.63 = f32[1,5,16,4096]{2,0,1,3:T(1,128)} copy(f32[1,5,16,4096]{3,2,1,0:T(8,128)S(1)} %pad_maximum_fusion) | data formatting | bytes 2621440 | tf_op jit(solution)/shard_map/concatenate | solution.py:78
  17.4 34.3 %reduce.12 = f32[4096,5,16]{2,1,0:T(8,128)} reduce(f32[4096,5,1,16]{3,2,1,0:T(1,128)} %bitcast.52, f32[]{:T(128)} %broadcast.383), dimensions={2}, to_apply=%bitcast.41.reduce_sub_computation | reduce | bytes 2621444
  51.7 9.3 %reshape.473 = f32[4,1,81920]{2,1,0:T(1,128)} reshape(f32[4096,5,16]{2,1,0:T(8,128)} %reduce.12) | data formatting | bytes 2621440
  61.0 4.2 %all-to-all-start = ((f32[4,1,81920]{2,1,0:T(1,128)}), f32[4,1,81920]{2,1,0:T(1,128)S(1)}, u32[]{:S(2)}, u32[]{:S(2)}) async-start(f32[4,1,81920]{2,1,0:T(1,128)} %reshape.473), calls=%async_computation | async-start | bytes 2621440 | tf_op jit(solution)/shard_map/all_to_all | solution.py:84
  69.4 1.7 fusion.35
  73.0 31.8 %all-gather = f32[8,5,16,1]{2,3,1,0:T(1,128)S(1)} all-gather(f32[1,5,16,1]{2,3,1,0:T(1,128)S(1)} %copy.75), channel_id=2, replica_groups=mesh['blk'=8,'line'=4] {'blk'}, dimensions={0}, use_global_device_ids=true | all-gather | bytes 2880 | tf_op jit(solution)/shard_map/all_gather | solution.py:92
  106.5 2.2 %fusion.46 = f32[1,3,16,4102]{3,2,1,0:T(8,128)} fusion(f32[1,5,16,4096]{3,2,1,0:T(8,128)S(1)} %copy-done.1, f32[3]{0:T(128)S(1)} %compare_convert_fusion, f32[16,4102]{1,0:T(8,128)} %get-tuple-element.45, f32[16,4102]{1,0:T(8,128)} %get-tuple-element.43), kind=kLoop, calls=%fused_computation.96 | loop fusion | flops 590688 | bytes 2623372 | tf_op jit(solution)/shard_map/add | solution.py:61
  108.7 1.7 slice_multiply_fusion.3
  110.4 5.5 %reduce.13 = f32[4,81920]{1,0:T(4,128)} reduce(f32[4,1,81920]{2,1,0:T(1,128)S(1)} %all-to-all-done, f32[]{:T(128)} %broadcast.383), dimensions={1}, to_apply=%all_to_all.26.reduce_sub_computation | reduce | bytes 2621444 | tf_op jit(solution)/shard_map/all_to_all | solution.py:84
  115.9 27.3 %reshape.474 = f32[4096,5,1,16]{3,2,1,0:T(1,128)} reshape(f32[4,81920]{1,0:T(4,128)} %reduce.13) | data formatting | bytes 2621440
  143.1 19.8 %copy.64 = f32[1,5,16,4096]{3,2,1,0:T(8,128)} copy(f32[1,5,16,4096]{2,0,1,3:T(1,128)} %bitcast.53) | data formatting | bytes 2621440 | tf_op jit(solution)/shard_map/all_to_all | solution.py:84
  162.9 2.2 %all_to_all.27 = f32[1,5,16,4,1024]{4,3,2,1,0:T(4,128)S(1)} reshape(f32[1,5,16,4096]{3,2,1,0:T(8,128)} %copy.64) | data formatting | bytes 2621440 | tf_op jit(solution)/shard_map/all_to_all | solution.py:84
  166.8 1.5 fusion.20
  169.1 1.4 fusion.12
  170.5 2.4 %copy.66 = f32[1,5,64,1024]{3,0,1,2:T(1,128)} copy(f32[1,5,64,1024]{3,2,1,0:T(8,128)S(1)} %fusion.12) | data formatting | bytes 2621440 | tf_op jit(solution)/shard_map/jit(_where)/select_n | solution.py:35
  172.9 4.3 %all-to-all-start.1 = ((f32[1,5,64,1024]{3,0,1,2:T(1,128)}), f32[1,5,64,1024]{3,0,1,2:T(1,128)}, u32[]{:S(2)}, u32[]{:S(2)}) async-start(f32[1,5,64,1024]{3,0,1,2:T(1,128)} %copy.66), calls=%async_computation.1 | async-start | bytes 2621440 | tf_op jit(solution)/shard_map/all_to_all | solution.py:87
  177.2 1.6 maximum_subtract_fusion.1
  178.7 15.7 %all-to-all-done.1 = f32[1,5,64,1024]{3,0,1,2:T(1,128)} async-done(((f32[1,5,64,1024]{3,0,1,2:T(1,128)}), f32[1,5,64,1024]{3,0,1,2:T(1,128)}, u32[]{:S(2)}, u32[]{:S(2)}) %all-to-all-start.1) | async-done | bytes 1310752 | tf_op jit(solution)/shard_map/all_to_all | solution.py:87
  194.5 1.6 copy.67
  196.2 2.1 fusion.6
  199.4 1.8 scatter-add.4
  201.2 2.7 %multiply_reduce_fusion = f32[]{:T(128)} fusion(f32[1,5,16,4096]{3,2,1,0:T(8,128)} %param.14, f32[1,5,16,4096]{3,2,1,0:T(8,128)} %scatter-add.4), kind=kLoop, calls=%fused_computation.50 | loop fusion | flops 655359 | bytes 2621444 | tf_op jit(solution)/shard_map/reduce_sum | solution.py:108
  203.9 6.4 %psum.7 = f32[]{:T(128)} all-reduce(f32[]{:T(128)} %multiply_reduce_fusion), channel_id=1, replica_groups=mesh['blk'=8,'line'=4] {'line'}, use_global_device_ids=true, to_apply=%region_5.6 | all-reduce | flops 1 | bytes 8 | tf_op jit(solution)/shard_map/psum | solution.py:108
  (56 shorter events, 11.1 us)
Async XLA Ops:
  2.0 66.1 %copy-start = (f32[1,5,16,4096]{3,2,1,0:T(8,128)}, f32[1,5,16,4096]{3,2,1,0:T(8,128)S(1)}, u32[]{:S(2)}) copy-start(f32[1,5,16,4096]{3,2,1,0:T(8,128)S(1)} %pad_maximum_fusion) | copy-start | bytes 3932164
  61.0 49.3 %all-to-all-start = ((f32[4,1,81920]{2,1,0:T(1,128)}), f32[4,1,81920]{2,1,0:T(1,128)S(1)}, u32[]{:S(2)}, u32[]{:S(2)}) async-start(f32[4,1,81920]{2,1,0:T(1,128)} %reshape.473), calls=%async_computation | async-start | bytes 2621440 | tf_op jit(solution)/shard_map/all_to_all | solution.py:84
  71.2 1.0 copy-start.3
  72.1 0.8 slice-start
  72.1 33.3 %copy-start.7 = (s32[1,4]{1,0:T(1,128)S(1)}, s32[1,4]{1,0:T(1,128)}, u32[]{:S(2)}) copy-start(s32[1,4]{1,0:T(1,128)} %param.17) | copy-start | bytes 52
  72.1 34.0 %copy-start.8 = (s32[1,4]{1,0:T(1,128)S(1)}, s32[1,4]{1,0:T(1,128)}, u32[]{:S(2)}) copy-start(s32[1,4]{1,0:T(1,128)} %param.15) | copy-start | bytes 52
  72.1 34.3 %copy-start.1 = (f32[1,5,16,4096]{3,2,1,0:T(8,128)S(1)}, f32[1,5,16,4096]{3,2,1,0:T(8,128)}, u32[]{:S(2)}) copy-start(f32[1,5,16,4096]{3,2,1,0:T(8,128)} %copy-done) | copy-start | bytes 3932164
  166.2 0.7 copy-start.4
  166.2 0.7 copy-start.5
  166.2 0.7 copy-start.6
  172.9 21.6 %all-to-all-start.1 = ((f32[1,5,64,1024]{3,0,1,2:T(1,128)}), f32[1,5,64,1024]{3,0,1,2:T(1,128)}, u32[]{:S(2)}, u32[]{:S(2)}) async-start(f32[1,5,64,1024]{3,0,1,2:T(1,128)} %copy.66), calls=%async_computation.1 | async-start | bytes 2621440 | tf_op jit(solution)/shard_map/all_to_all | solution.py:87
  198.3 1.1 copy-start.2
where the time goes:
time: 213 us; the launch traced here: 212 us
  local copies, waits for them, and re-layouts  84.1 us (39%)
  other arithmetic  61.9 us (29%)
  blocking collectives  38.1 us (18%)
  waiting for transfers between devices  15.7 us (7%)
  starting transfers between devices  8.53 us (4%)
  between operations  3.44 us (2%)
    unnamed x22, local copies, waits for them, and re-layouts  39.8 us
    unnamed x1, other arithmetic  34.3 us
    all_gather x1, blocking collectives, per_device(): gathered = lax.all_gather(bottom_row, 'blk', axis=0, tiled=True)  31.8 us
    all_to_all x3, local copies, waits for them, and re-layouts, per_device(): lax.all_to_all(state, 'line', split_axis=3, concat_axis=2, tiled=True)  22.7 us
    all_to_all x1, waiting for transfers between devices, per_device(): lax.all_to_all(line_part, 'line', split_axis=2, concat_axis=3, tiled=True)  15.7 us
    concatenate x1, local copies, waits for them, and re-layouts, per_device(): jnp.concatenate([density[:, None], momentum, energy[:, None]], axis=1)  14.9 us
    psum x1, blocking collectives, per_device(): total = lax.psum(jnp.sum(adjoint * result), 'line')  6.37 us
    all_to_all x1, other arithmetic, per_device(): lax.all_to_all(state, 'line', split_axis=3, concat_axis=2, tiled=True)  5.48 us
  transfers between devices with their start and end apart: 2, of which 1 were waited for; matrix products, arithmetic and copies ran while one was open for 6% of the time, Pallas kernels for 0%

commit v1 on v0

--- a/solution.py
+++ b/solution.py
@@ -10,6 +10,23 @@
 viscosity = 0.5
 conduction = 1.5
 penalty = 4.0
+
+
+def in_order(tiles, dim):
+    tiles = jnp.moveaxis(tiles, 0, dim)
+    lengths = tiles.shape
+    return tiles.reshape(*lengths[:dim], lengths[dim] * lengths[dim + 1], *lengths[dim + 2 :])
+
+
+def gather_around(x, axis, dim):
+    size = lax.axis_size(axis)
+    right = [(i, (i + 1) % size) for i in range(size)]
+    blocks = [x]
+    while len(blocks) < size:
+        blocks.append(lax.ppermute(blocks[-1], axis, right))
+    position = lax.axis_index(axis)
+    blocks = jnp.stack(blocks)[(position - jnp.arange(size)) % size]
+    return in_order(blocks, dim)
 
 
 def difference(fields, direction, start_row, extent):
@@ -89,7 +106,7 @@
     ypart = direction_residual(padded_y, 3, -6, yextent, 1)
     result = xpart + ypart
     bottom_row = state[:, :, :, 0]
-    gathered = lax.all_gather(bottom_row, "blk", axis=0, tiled=True)
+    gathered = gather_around(bottom_row, "blk", 0)
     slots = jnp.arange(partners.shape[1], dtype=jnp.int32)
     listed = partners[0]
     count_here = counts[0]

time: 213 us -> 204 us (0.958)
  blocking collectives: 38.1 us -> 6.37 us
  waiting for transfers between devices: 15.7 us -> 33.3 us
  starting transfers between devices: 8.53 us -> 13.7 us
  other arithmetic: 61.9 us -> 59.7 us
    all_gather x1 -> x0, blocking collectives: 31.8 us -> none  [per_device(): gathered = lax.all_gather(bottom_row, 'blk', axis=0, tiled=True)]
    ppermute x0 -> x7, waiting for transfers between devices: none -> 29.9 us  [gather_around(): blocks.append(lax.ppermute(blocks[-1], axis, right))]
    all_to_all x1, waiting for transfers between devices: 15.7 us -> 3.45 us  [per_device(): lax.all_to_all(line_part, 'line', split_axis=2, concat_axis=3, tiled=True)]
    ppermute x0 -> x7, starting transfers between devices: none -> 4.69 us  [gather_around(): blocks.append(lax.ppermute(blocks[-1], axis, right))]
    all_to_all x3, local copies, waits for them, and re-layouts: 22.7 us -> 24.9 us  [per_device(): lax.all_to_all(state, 'line', split_axis=3, concat_axis=2, tiled=True)]
    unnamed x22 -> x28, local copies, waits for them, and re-layouts: 39.8 us -> 39.9 us
  transfers between devices with their start and end apart: 2 -> 9, of which waited for: 1 -> 6; matrix products, arithmetic and copies ran while one was open for 6% -> 35% of each run, Pallas kernels for 0% -> 0%
where the time goes in v1:
time: 204 us; the launch traced here: 203 us
  local copies, waits for them, and re-layouts  86.1 us (42%)
  other arithmetic  59.7 us (29%)
  waiting for transfers between devices  33.3 us (16%)
  starting transfers between devices  13.7 us (7%)
  blocking collectives  6.37 us (3%)
  between operations  3.49 us (2%)
    unnamed x28, local copies, waits for them, and re-layouts  39.9 us
    unnamed x1, other arithmetic  35.5 us
    ppermute x7, waiting for transfers between devices, gather_around(): blocks.append(lax.ppermute(blocks[-1], axis, right))  29.9 us
    all_to_all x3, local copies, waits for them, and re-layouts, per_device(): lax.all_to_all(state, 'line', split_axis=3, concat_axis=2, tiled=True)  24.9 us
    concatenate x1, local copies, waits for them, and re-layouts, per_device(): jnp.concatenate([density[:, None], momentum, energy[:, None]], axis=1)  14.7 us
    all_to_all x1, other arithmetic, per_device(): lax.all_to_all(state, 'line', split_axis=3, concat_axis=2, tiled=True)  6.44 us
    psum x1, blocking collectives, per_device(): total = lax.psum(jnp.sum(adjoint * result), 'line')  6.37 us
    ppermute x7, starting transfers between devices, gather_around(): blocks.append(lax.ppermute(blocks[-1], axis, right))  4.69 us
  transfers between devices with their start and end apart: 9, of which 6 were waited for; matrix products, arithmetic and copies ran while one was open for 35% of the time, Pallas kernels for 0%

profile of v1, /device:TPU:0, one launch (start us, length us, event | category | flops | bytes accessed | tf_op | source)
XLA Modules:
  0.0 202.9 jit_solution(4248050468235166495)
XLA Ops:
  2.0 14.7 %copy.61 = f32[1,5,16,4096]{2,0,1,3:T(1,128)} copy(f32[1,5,16,4096]{3,2,1,0:T(8,128)S(1)} %pad_maximum_fusion) | data formatting | bytes 2621440 | tf_op jit(solution)/shard_map/concatenate | solution.py:95
  17.3 35.5 %reduce.15 = f32[4096,5,16]{2,1,0:T(8,128)} reduce(f32[4096,5,1,16]{3,2,1,0:T(1,128)} %bitcast.83, f32[]{:T(128)} %broadcast.454), dimensions={2}, to_apply=%bitcast.71.reduce_sub_computation | reduce | bytes 2621444
  52.8 9.3 %reshape.538 = f32[4,1,81920]{2,1,0:T(1,128)} reshape(f32[4096,5,16]{2,1,0:T(8,128)} %reduce.15) | data formatting | bytes 2621440
  62.0 4.3 %all-to-all-start = ((f32[4,1,81920]{2,1,0:T(1,128)}), f32[4,1,81920]{2,1,0:T(1,128)}, u32[]{:S(2)}, u32[]{:S(2)}) async-start(f32[4,1,81920]{2,1,0:T(1,128)} %reshape.538), calls=%async_computation | async-start | bytes 2621440 | tf_op jit(solution)/shard_map/all_to_all | solution.py:101
  66.4 3.0 %collective-permute-start = (f32[1,5,16]{2,0,1:T(1,128)S(1)}, f32[1,5,16]{2,0,1:T(1,128)S(1)}, u32[]{:S(2)}, u32[]{:S(2)}) collective-permute-start(f32[1,5,16]{2,0,1:T(1,128)S(1)} %squeeze.9), channel_id=1, source_target_pairs={{0,4},{4,8},{8,12},{12,16},{16,20},{20,24},{24,28},{28,0},{1,5},{5... | collective-permute-start | bytes 968 | tf_op jit(solution)/shard_map/ppermute | solution.py:26
  71.5 1.7 fusion.35
  80.7 4.8 %collective-permute-done.1 = f32[1,5,16]{2,0,1:T(1,128)S(1)} collective-permute-done((f32[1,5,16]{2,0,1:T(1,128)S(1)}, f32[1,5,16]{2,0,1:T(1,128)S(1)}, u32[]{:S(2)}, u32[]{:S(2)}) %collective-permute-start.1) | collective-permute-done | bytes 352 | tf_op jit(solution)/shard_map/ppermute | solution.py:26
  85.5 6.3 %collective-permute-done.2 = f32[1,5,16]{2,0,1:T(1,128)S(1)} collective-permute-done((f32[1,5,16]{2,0,1:T(1,128)S(1)}, f32[1,5,16]{2,0,1:T(1,128)S(1)}, u32[]{:S(2)}, u32[]{:S(2)}) %collective-permute-start.2) | collective-permute-done | bytes 352 | tf_op jit(solution)/shard_map/ppermute | solution.py:26
  91.8 6.3 %collective-permute-done.3 = f32[1,5,16]{2,0,1:T(1,128)S(1)} collective-permute-done((f32[1,5,16]{2,0,1:T(1,128)S(1)}, f32[1,5,16]{2,0,1:T(1,128)S(1)}, u32[]{:S(2)}, u32[]{:S(2)}) %collective-permute-start.3) | collective-permute-done | bytes 352 | tf_op jit(solution)/shard_map/ppermute | solution.py:26
  98.1 6.4 %reduce.16 = f32[4,81920]{1,0:T(4,128)} reduce(f32[4,1,81920]{2,1,0:T(1,128)} %all-to-all-done, f32[]{:T(128)} %broadcast.454), dimensions={1}, to_apply=%all_to_all.26.reduce_sub_computation | reduce | bytes 2621444 | tf_op jit(solution)/shard_map/all_to_all | solution.py:101
  104.5 27.3 %reshape.539 = f32[4096,5,1,16]{3,2,1,0:T(1,128)} reshape(f32[4,81920]{1,0:T(4,128)} %reduce.16) | data formatting | bytes 2621440
  131.8 19.8 %copy.62 = f32[1,5,16,4096]{3,2,1,0:T(8,128)} copy(f32[1,5,16,4096]{2,0,1,3:T(1,128)} %bitcast.84) | data formatting | bytes 2621440 | tf_op jit(solution)/shard_map/all_to_all | solution.py:101
  151.6 3.0 %all_to_all.27 = f32[1,5,16,4,1024]{4,3,2,1,0:T(4,128)} reshape(f32[1,5,16,4096]{3,2,1,0:T(8,128)} %copy.62) | data formatting | bytes 2621440 | tf_op jit(solution)/shard_map/all_to_all | solution.py:101
  154.6 2.1 %copy.63 = f32[1,5,4,16,1024]{4,3,2,1,0:T(8,128)S(1)} copy(f32[1,5,4,16,1024]{4,2,3,1,0:T(4,128)} %bitcast.85) | data formatting | bytes 2621440 | tf_op jit(solution)/shard_map/all_to_all | solution.py:101
  161.3 2.4 %copy.64 = f32[1,5,64,1024]{3,0,1,2:T(1,128)} copy(f32[1,5,64,1024]{3,2,1,0:T(8,128)S(1)} %fusion.12) | data formatting | bytes 2621440 | tf_op jit(solution)/shard_map/jit(_where)/select_n | solution.py:52
  163.7 4.7 %all-to-all-start.1 = ((f32[1,5,64,1024]{3,0,1,2:T(1,128)}), f32[1,5,64,1024]{3,0,1,2:T(1,128)}, u32[]{:S(2)}, u32[]{:S(2)}) async-start(f32[1,5,64,1024]{3,0,1,2:T(1,128)} %copy.64), calls=%async_computation.1 | async-start | bytes 2621440 | tf_op jit(solution)/shard_map/all_to_all | solution.py:104
  168.5 6.3 %collective-permute-done.5 = f32[1,5,16]{2,0,1:T(1,128)S(1)} collective-permute-done((f32[1,5,16]{2,0,1:T(1,128)S(1)}, f32[1,5,16]{2,0,1:T(1,128)S(1)}, u32[]{:S(2)}, u32[]{:S(2)}) %collective-permute-start.5) | collective-permute-done | bytes 352 | tf_op jit(solution)/shard_map/ppermute | solution.py:26
  174.8 6.3 %collective-permute-done.6 = f32[1,5,16]{2,0,1:T(1,128)S(1)} collective-permute-done((f32[1,5,16]{2,0,1:T(1,128)S(1)}, f32[1,5,16]{2,0,1:T(1,128)S(1)}, u32[]{:S(2)}, u32[]{:S(2)}) %collective-permute-start.6) | collective-permute-done | bytes 352 | tf_op jit(solution)/shard_map/ppermute | solution.py:26
  182.0 3.4 %all-to-all-done.1 = f32[1,5,64,1024]{3,0,1,2:T(1,128)} async-done(((f32[1,5,64,1024]{3,0,1,2:T(1,128)}), f32[1,5,64,1024]{3,0,1,2:T(1,128)}, u32[]{:S(2)}, u32[]{:S(2)}) %all-to-all-start.1) | async-done | bytes 1310752 | tf_op jit(solution)/shard_map/all_to_all | solution.py:104
  185.4 1.6 copy.65
  187.1 2.1 %fusion.6 = f32[1,5,16,4096]{3,2,1,0:T(8,128)S(1)} fusion(f32[1,5,16,4096]{3,2,1,0:T(8,128)S(1)} %bitcast.87, f32[1,5,16,4102]{3,2,1,0:T(8,128)S(1)} %maximum_subtract_fusion.1, pred[4096]{0:T(1024)(128)(4,1)S(1)} %get-tuple-element.59, pred[4096]{0:T(1024)(128)(4,1)S(1)} %get-tuple-element.58, pred[4096]{0:T(1024)(128)(4,1)S(1)} %get-tuple-element.56, ...), kind=kLoop, calls=%fused_computation.40 | loop fusion | flops 6225920 | bytes 11812864 | tf_op jit(solution)/shard_map/add | solution.py:107
  190.4 1.8 scatter-add.4
  192.2 2.7 %multiply_reduce_fusion = f32[]{:T(128)} fusion(f32[1,5,16,4096]{3,2,1,0:T(8,128)} %param.14, f32[1,5,16,4096]{3,2,1,0:T(8,128)} %scatter-add.4), kind=kLoop, calls=%fused_computation.51 | loop fusion | flops 655359 | bytes 2621444 | tf_op jit(solution)/shard_map/reduce_sum | solution.py:125
  194.8 6.4 %psum.7 = f32[]{:T(128)} all-reduce(f32[]{:T(128)} %multiply_reduce_fusion), channel_id=1, replica_groups=mesh['blk'=8,'line'=4] {'line'}, use_global_device_ids=true, to_apply=%region_5.6 | all-reduce | flops 1 | bytes 8 | tf_op jit(solution)/shard_map/psum | solution.py:125
  (80 shorter events, 17.4 us)
Async XLA Ops:
  62.0 36.0 %all-to-all-start = ((f32[4,1,81920]{2,1,0:T(1,128)}), f32[4,1,81920]{2,1,0:T(1,128)}, u32[]{:S(2)}, u32[]{:S(2)}) async-start(f32[4,1,81920]{2,1,0:T(1,128)} %reshape.538), calls=%async_computation | async-start | bytes 2621440 | tf_op jit(solution)/shard_map/all_to_all | solution.py:101
  66.4 12.7 %collective-permute-start = (f32[1,5,16]{2,0,1:T(1,128)S(1)}, f32[1,5,16]{2,0,1:T(1,128)S(1)}, u32[]{:S(2)}, u32[]{:S(2)}) collective-permute-start(f32[1,5,16]{2,0,1:T(1,128)S(1)} %squeeze.9), channel_id=1, source_target_pairs={{0,4},{4,8},{8,12},{12,16},{16,20},{20,24},{24,28},{28,0},{1,5},{5... | collective-permute-start | bytes 968 | tf_op jit(solution)/shard_map/ppermute | solution.py:26
  76.7 1.0 copy-start.1
  76.7 1.0 copy-start.2
  76.7 1.1 copy-start.3
  77.8 0.7 copy-start.7
  79.2 6.3 %collective-permute-start.1 = (f32[1,5,16]{2,0,1:T(1,128)S(1)}, f32[1,5,16]{2,0,1:T(1,128)S(1)}, u32[]{:S(2)}, u32[]{:S(2)}) collective-permute-start(f32[1,5,16]{2,0,1:T(1,128)S(1)} %collective-permute-done), channel_id=1, source_target_pairs={{0,4},{4,8},{8,12},{12,16},{16,20},{20,24},{24,28},{28,0},{1,5},{5... | collective-permute-start | bytes 968 | tf_op jit(solution)/shard_map/ppermute | solution.py:26
  85.5 6.3 %collective-permute-start.2 = (f32[1,5,16]{2,0,1:T(1,128)S(1)}, f32[1,5,16]{2,0,1:T(1,128)S(1)}, u32[]{:S(2)}, u32[]{:S(2)}) collective-permute-start(f32[1,5,16]{2,0,1:T(1,128)S(1)} %collective-permute-done.1), channel_id=1, source_target_pairs={{0,4},{4,8},{8,12},{12,16},{16,20},{20,24},{24,28},{28,0},{1,5},{5... | collective-permute-start | bytes 968 | tf_op jit(solution)/shard_map/ppermute | solution.py:26
  91.8 6.3 %collective-permute-start.3 = (f32[1,5,16]{2,0,1:T(1,128)S(1)}, f32[1,5,16]{2,0,1:T(1,128)S(1)}, u32[]{:S(2)}, u32[]{:S(2)}) collective-permute-start(f32[1,5,16]{2,0,1:T(1,128)S(1)} %collective-permute-done.2), channel_id=1, source_target_pairs={{0,4},{4,8},{8,12},{12,16},{16,20},{20,24},{24,28},{28,0},{1,5},{5... | collective-permute-start | bytes 968 | tf_op jit(solution)/shard_map/ppermute | solution.py:26
  98.1 70.3 %collective-permute-start.4 = (f32[1,5,16]{2,0,1:T(1,128)S(1)}, f32[1,5,16]{2,0,1:T(1,128)S(1)}, u32[]{:S(2)}, u32[]{:S(2)}) collective-permute-start(f32[1,5,16]{2,0,1:T(1,128)S(1)} %collective-permute-done.3), channel_id=1, source_target_pairs={{0,4},{4,8},{8,12},{12,16},{16,20},{20,24},{24,28},{28,0},{1,5},{5... | collective-permute-start | bytes 968 | tf_op jit(solution)/shard_map/ppermute | solution.py:26
  157.0 0.7 copy-start.4
  157.0 0.7 copy-start.5
  157.0 0.7 copy-start.6
  163.7 17.9 %copy-start.8 = (s32[1,4]{1,0:T(1,128)S(1)}, s32[1,4]{1,0:T(1,128)}, u32[]{:S(2)}) copy-start(s32[1,4]{1,0:T(1,128)} %param.15) | copy-start | bytes 52
  163.7 21.7 %all-to-all-start.1 = ((f32[1,5,64,1024]{3,0,1,2:T(1,128)}), f32[1,5,64,1024]{3,0,1,2:T(1,128)}, u32[]{:S(2)}, u32[]{:S(2)}) async-start(f32[1,5,64,1024]{3,0,1,2:T(1,128)} %copy.64), calls=%async_computation.1 | async-start | bytes 2621440 | tf_op jit(solution)/shard_map/all_to_all | solution.py:104
  168.4 6.3 %collective-permute-start.5 = (f32[1,5,16]{2,0,1:T(1,128)S(1)}, f32[1,5,16]{2,0,1:T(1,128)S(1)}, u32[]{:S(2)}, u32[]{:S(2)}) collective-permute-start(f32[1,5,16]{2,0,1:T(1,128)S(1)} %collective-permute-done.4), channel_id=1, source_target_pairs={{0,4},{4,8},{8,12},{12,16},{16,20},{20,24},{24,28},{28,0},{1,5},{5... | collective-permute-start | bytes 968 | tf_op jit(solution)/shard_map/ppermute | solution.py:26
  174.8 6.3 %collective-permute-start.6 = (f32[1,5,16]{2,0,1:T(1,128)S(1)}, f32[1,5,16]{2,0,1:T(1,128)S(1)}, u32[]{:S(2)}, u32[]{:S(2)}) collective-permute-start(f32[1,5,16]{2,0,1:T(1,128)S(1)} %collective-permute-done.5), channel_id=1, source_target_pairs={{0,4},{4,8},{8,12},{12,16},{16,20},{20,24},{24,28},{28,0},{1,5},{5... | collective-permute-start | bytes 968 | tf_op jit(solution)/shard_map/ppermute | solution.py:26
  189.2 1.1 copy-start
